TPU v7x, 512 devices: a whole 4x4x16 slice. The times are simulated.
512 devices in a mesh: row: 16 (over y, x), col: 32 (over z, core).
Axes of the slice: x: 4, y: 4, z: 16, core: 2. Of those that a mesh axis runs over, the one named last changes fastest.
Arguments:
- panel: bfloat16 [4, 16, 512, 512], P(None, 'row', 'col'), may hold values from -1.1953125 to 1.1953125
- inverse_factor: bfloat16 [512, 512], replicated
- slot_rows: int32 [16, 32, 2], P('row', 'col'), may hold values from 0 to 63, as said below
- slot_cols: int32 [16, 32, 2], P('row', 'col'), may hold values from 0 to 63, as said below
- live_count: int32 [16, 32], P('row', 'col'), may hold values from 0 to 2
Outputs:
- contrib: bfloat16 [16, 32, 2, 512, 512], P('row', 'col')
Inputs may be any that keep to these rules, and one draw needn't show every extreme that they name: slot_rows[r, c, s] is congruent to r modulo 16; for s < live_count[r, c] the slots of one position name distinct blocks with slot_rows >= slot_cols; the other slots are ignored. slot_cols[r, c, s] is congruent to c modulo 32.
All inputs are finite; a program needn't handle non-finite values.
Results may differ from a plain program's by a relative error of at most 0.0054.
Values may be sent and summed in bfloat16 or wider, within the bound.
No kernel may reach another device: no remote copies, remote signals or barrier semaphores. Data moves between devices by JAX's collectives and lax.ppermute only.
A program may use at most 64 MiB of HBM per device.

v0:
```python
import jax
import jax.numpy as jnp
from jax import lax
from jax.sharding import PartitionSpec as P


def broadcast(value, axis, source):
    kept = jnp.where(lax.axis_index(axis) == source, value, 0).astype(value.dtype)
    return lax.psum(kept, axis)


def body(panel, inverse_factor, slot_rows, slot_cols, live_count):
    panel_count, _, part_rows, tile_width = panel.shape
    grid_rows = lax.axis_size("row")
    grid_cols = lax.axis_size("col")
    col_ratio = grid_cols // grid_rows
    column_count = panel_count // col_ratio
    solved = jnp.dot(
        panel.reshape(-1, tile_width), inverse_factor, preferred_element_type=jnp.float32
    )
    solved = solved.astype(jnp.bfloat16).reshape(panel_count, 1, part_rows, tile_width)
    row_blocks = lax.all_gather(solved, "col", axis=2, tiled=True).reshape(
        panel_count, tile_width, tile_width
    )
    position = lax.axis_index("col")
    grouped = row_blocks.reshape(column_count, col_ratio, tile_width, tile_width)
    picked = lax.dynamic_index_in_dim(grouped, position // grid_rows, 1, keepdims=False)
    col_blocks = broadcast(picked, "row", position % grid_rows)
    slot_total = slot_rows.shape[-1]
    rows_here = slot_rows.reshape(-1)
    cols_here = slot_cols.reshape(-1)
    live_here = live_count.reshape(())
    result = jnp.zeros((slot_total, tile_width, tile_width), jnp.bfloat16)

    def update(slot, current):
        left_tile = lax.dynamic_index_in_dim(
            row_blocks, rows_here[slot] // grid_rows, 0, keepdims=False
        )
        right_tile = lax.dynamic_index_in_dim(
            col_blocks, cols_here[slot] // grid_cols, 0, keepdims=False
        )
        product = lax.dot_general(
            left_tile, right_tile, (((1,), (1,)), ((), ())), preferred_element_type=jnp.float32
        )
        return lax.dynamic_update_index_in_dim(current, (-product).astype(jnp.bfloat16), slot, 0)

    result = lax.fori_loop(0, live_here, update, result)
    return result.reshape(1, 1, slot_total, tile_width, tile_width)


def solution(mesh):
    placed = (
        P(None, "row", "col", None),
        P(),
        P("row", "col", None),
        P("row", "col", None),
        P("row", "col"),
    )
    return jax.shard_map(
        body,
        mesh=mesh,
        in_specs=placed,
        out_specs=P("row", "col", None, None, None),
        check_vma=False,
    )
```

profile of v0, /device:TPU:32, one launch (start us, length us, event | category | flops | bytes accessed | tf_op | source)
XLA Modules:
  0.0 229.6 jit_solution(7024908279362446910)
XLA Ops:
  6.5 0.0 copy-start
  6.5 0.0 all-gather.2.cloned.1.call-start
  6.5 1.0 copy-done
  7.6 1.7 convolution_convert_fusion
  9.3 0.0 all-gather.2.cloned.1.call-update
  9.3 0.0 all-reduce.2.cloned.1.call-start
  9.4 76.0 %all-gather.2.cloned.1.call-done = bf16[4,1,512,512]{3,2,0,1:T(8,128)(2,1)} async-done(((bf16[4,1,16,512]{3,2,0,1:T(8,128)(2,1)}), bf16[4,1,512,512]{3,2,0,1:T(8,128)(2,1)}) %all-gather.2.cloned.1.call-update) | async-done | bytes 2097168 | tf_op jit(solution)/shard_map/all_gather | solution.py:22
  85.3 0.0 copy-start.2
  85.3 0.0 copy-start.3
  85.3 2.3 select_bitcast_fusion
  87.6 0.0 all-reduce.2.cloned.1.call-update
  87.7 115.9 %all-reduce.2.cloned.1.call-done = bf16[2,512,512]{2,1,0:T(8,128)(2,1)} async-done(((bf16[2,512,512]{2,1,0:T(8,128)(2,1)}), bf16[2,512,512]{2,1,0:T(8,128)(2,1)}) %all-reduce.2.cloned.1.call-update) | async-done | bytes 1048592 | tf_op jit(solution)/shard_map/psum | solution.py:9
  203.6 0.1 broadcast_in_dim.15
  203.6 0.0 copy-done.2
  203.6 0.0 copy-done.3
  203.7 18.1 %while.13 = (s32[]{:T(128)}, bf16[2,512,512]{2,1,0:T(8,128)(2,1)S(1)}, s32[]{:T(128)}, s32[2]{0:T(128)S(1)}, bf16[4,512,512]{2,1,0:T(8,128)(2,1)}, /*index=5*/s3...) while((s32[]{:T(128)}, ...), condition=%wide.region_2.3_spmd, body=%wide.region_1.2_spmd.sunk | while | flops 268959776 | bytes 1573451 | solution.py:47
  204.3 0.6 dynamic_slice.51
  207.5 0.6 dynamic_slice.50
  210.7 1.7 fusion.15
  213.1 0.6 dynamic_slice.51
  216.3 0.6 dynamic_slice.50
  219.5 1.7 fusion.15
  221.8 0.0 copy-start.1
  221.8 1.0 copy-done.1
Async XLA Ops:
  6.5 1.0 copy-start
  6.5 78.8 %all-gather.2.cloned.1.call-start = ((), (), s32[]{:S(2)}) async-start(), calls=%async_computation | async-start | bytes 2162688 | tf_op jit(solution)/shard_map/all_gather | solution.py:22
  9.3 194.3 %all-reduce.2.cloned.1.call-start = ((), (), s32[]{:S(2)}) async-start(), calls=%async_computation.1 | async-start | bytes 2097152 | tf_op jit(solution)/shard_map/psum | solution.py:9
  85.3 118.3 %copy-start.2 = (s32[1,1,2]{2,1,0:T(1,128)S(1)}, s32[1,1,2]{2,1,0:T(1,128)}, u32[]{:S(2)}) copy-start(s32[1,1,2]{2,1,0:T(1,128)} %param.9) | copy-start | bytes 28
  85.3 118.3 %copy-start.3 = (s32[1,1,2]{2,1,0:T(1,128)S(1)}, s32[1,1,2]{2,1,0:T(1,128)}, u32[]{:S(2)}) copy-start(s32[1,1,2]{2,1,0:T(1,128)} %param.10) | copy-start | bytes 28
  221.8 1.0 copy-start.1
Sparse Core Ops, SparseCore 0:
  9.5 75.7 all-gather.1
  88.6 114.9 all-reduce.1
where the time goes:
time: 230 us
  waiting for transfers between devices  192 us (83%)
  between operations  13.5 us (6%)
  loops' own time  12.4 us (5%)
  matrix products  5.03 us (2%)
  local copies, waits for them, and re-layouts  4.43 us (2%)
    psum x1, waiting for transfers between devices, broadcast(): return lax.psum(kept, axis)  116 us
    all_gather x1, waiting for transfers between devices, body(): lax.all_gather(solved, 'col', axis=2, tiled=True)  76 us
    another operation x1, loops' own time, body(): result = lax.fori_loop(0, live_here, update, result)  12.4 us
  transfers between devices with their start and end apart: 2, of which 2 were waited for; matrix products, arithmetic and copies ran while one was open for 0% of the time, Pallas kernels for 0%

commit v1 on v0

--- a/solution.py
+++ b/solution.py
@@ -19,9 +19,9 @@
         panel.reshape(-1, tile_width), inverse_factor, preferred_element_type=jnp.float32
     )
     solved = solved.astype(jnp.bfloat16).reshape(panel_count, 1, part_rows, tile_width)
-    row_blocks = lax.all_gather(solved, "col", axis=2, tiled=True).reshape(
-        panel_count, tile_width, tile_width
-    )
+    row_blocks = jnp.concatenate(
+        lax.all_to_all(jnp.stack([solved] * lax.axis_size("col")), "col", 0, 0), axis=2
+    ).reshape(panel_count, tile_width, tile_width)
     position = lax.axis_index("col")
     grouped = row_blocks.reshape(column_count, col_ratio, tile_width, tile_width)
     picked = lax.dynamic_index_in_dim(grouped, position // grid_rows, 1, keepdims=False)

time: 230 us -> 265 us (1.15)
  waiting for transfers between devices: 192 us -> 210 us
  starting transfers between devices: 0.04 us -> 15.4 us
  local copies, waits for them, and re-layouts: 4.43 us -> 7.57 us
    all_to_all x0 -> x1, waiting for transfers between devices: none -> 100 us  [body(): lax.all_to_all(jnp.stack([solved] * lax.axis_size('col')), 'col', 0, 0)]
    all_gather x1 -> x0, waiting for transfers between devices: 76 us -> none  [body(): lax.all_gather(solved, 'col', axis=2, tiled=True)]
    all_to_all x0 -> x1, starting transfers between devices: none -> 15.4 us  [body(): lax.all_to_all(jnp.stack([solved] * lax.axis_size('col')), 'col', 0, 0)]
    psum x1, waiting for transfers between devices: 116 us -> 110 us  [broadcast(): return lax.psum(kept, axis)]
where the time goes in v1:
time: 265 us
  waiting for transfers between devices  210 us (79%)
  starting transfers between devices  15.4 us (6%)
  between operations  13.5 us (5%)
  loops' own time  12.4 us (5%)
  local copies, waits for them, and re-layouts  7.57 us (3%)
  matrix products  4.39 us (2%)
    psum x1, waiting for transfers between devices, broadcast(): return lax.psum(kept, axis)  110 us
    all_to_all x1, waiting for transfers between devices, body(): lax.all_to_all(jnp.stack([solved] * lax.axis_size('col')), 'col', 0, 0)  100 us
    all_to_all x1, starting transfers between devices, body(): lax.all_to_all(jnp.stack([solved] * lax.axis_size('col')), 'col', 0, 0)  15.4 us
    another operation x1, loops' own time, body(): result = lax.fori_loop(0, live_here, update, result)  12.4 us
  transfers between devices with their start and end apart: 2, of which 2 were waited for; matrix products, arithmetic and copies ran while one was open for 0% of the time, Pallas kernels for 0%

profile of v1, /device:TPU:32, one launch (start us, length us, event | category | flops | bytes accessed | tf_op | source)
XLA Modules:
  0.0 264.7 jit_solution(14646387160080373537)
XLA Ops:
  6.5 0.0 copy-start
  6.5 1.0 copy-done
  7.6 1.0 convolution_convert_fusion
  8.6 1.6 stack.3
  10.2 15.4 %all-to-all-start = ((bf16[32,4,1,16,512]{4,3,1,2,0:T(8,128)(2,1)}), bf16[32,4,1,16,512]{4,3,1,2,0:T(8,128)(2,1)S(1)}, u32[]{:S(2)}, u32[]{:S(2)}) async-start(bf16[32,4,1,16,512]{4,3,1,2,0:T(8,128)(2,1)} %stack.3), calls=%async_computation | async-start | bytes 4194304 | tf_op jit(solution)/shard_map/all_to_all | solution.py:23
  25.6 0.0 all-reduce.2.cloned.1.call-start
  25.7 100.1 %all-to-all-done = bf16[32,4,1,16,512]{4,3,1,2,0:T(8,128)(2,1)S(1)} async-done(((bf16[32,4,1,16,512]{4,3,1,2,0:T(8,128)(2,1)}), bf16[32,4,1,16,512]{4,3,1,2,0:T(8,128)(2,1)S(1)}, u32[]{:S(2)}, u32[]{:S(2)}) %all-to-all-start) | async-done | bytes 2097184 | tf_op jit(solution)/shard_map/all_to_all | solution.py:23
  125.7 0.2 copy.6
  125.9 0.0 copy-start.1
  125.9 1.3 copy-done.1
  127.3 1.0 select_bitcast_fusion
  128.3 0.0 all-reduce.2.cloned.1.call-update
  128.3 110.3 %all-reduce.2.cloned.1.call-done = bf16[2,512,512]{2,1,0:T(8,128)(2,1)} async-done(((bf16[2,512,512]{2,1,0:T(8,128)(2,1)}), bf16[2,512,512]{2,1,0:T(8,128)(2,1)}) %all-reduce.2.cloned.1.call-update) | async-done | bytes 1048592 | tf_op jit(solution)/shard_map/psum | solution.py:9
  238.7 0.1 broadcast_in_dim.15
  238.8 0.0 copy-done.3
  238.8 18.1 %while.13 = (s32[]{:T(128)}, bf16[2,512,512]{2,1,0:T(8,128)(2,1)S(1)}, s32[]{:T(128)}, s32[2]{0:T(128)S(1)}, bf16[4,512,512]{2,1,0:T(8,128)(2,1)}, /*index=5*/s3...) while((s32[]{:T(128)}, ...), condition=%wide.region_2.3_spmd, body=%wide.region_1.2_spmd.sunk | while | flops 268959776 | bytes 1573443 | solution.py:47
  239.5 0.6 dynamic_slice.51
  242.6 0.6 dynamic_slice.50
  245.8 1.7 fusion.15
  248.2 0.6 dynamic_slice.51
  251.4 0.6 dynamic_slice.50
  254.6 1.7 fusion.15
  256.9 0.0 copy-start.2
  256.9 1.0 copy-done.2
  (3 shorter events, 0.0 us)
Async XLA Ops:
  6.5 1.0 copy-start
  10.2 115.5 %all-to-all-start = ((bf16[32,4,1,16,512]{4,3,1,2,0:T(8,128)(2,1)}), bf16[32,4,1,16,512]{4,3,1,2,0:T(8,128)(2,1)S(1)}, u32[]{:S(2)}, u32[]{:S(2)}) async-start(bf16[32,4,1,16,512]{4,3,1,2,0:T(8,128)(2,1)} %stack.3), calls=%async_computation | async-start | bytes 4194304 | tf_op jit(solution)/shard_map/all_to_all | solution.py:23
  25.6 213.1 %all-reduce.2.cloned.1.call-start = ((), (), s32[]{:S(2)}) async-start(), calls=%async_computation.1 | async-start | bytes 2097152 | tf_op jit(solution)/shard_map/psum | solution.py:9
  125.9 1.3 copy-start.1
  127.3 111.5 %copy-start.3 = (s32[1,1,2]{2,1,0:T(1,128)S(1)}, s32[1,1,2]{2,1,0:T(1,128)}, u32[]{:S(2)}) copy-start(s32[1,1,2]{2,1,0:T(1,128)} %param.9) | copy-start | bytes 28
  127.3 111.5 %copy-start.4 = (s32[1,1,2]{2,1,0:T(1,128)S(1)}, s32[1,1,2]{2,1,0:T(1,128)}, u32[]{:S(2)}) copy-start(s32[1,1,2]{2,1,0:T(1,128)} %param.10) | copy-start | bytes 28
  256.9 1.0 copy-start.2
Sparse Core Ops, SparseCore 0:
  128.5 110.1 all-reduce.1

commit v2 on v0

--- a/solution.py
+++ b/solution.py
@@ -6,7 +6,7 @@
 
 def broadcast(value, axis, source):
     kept = jnp.where(lax.axis_index(axis) == source, value, 0).astype(value.dtype)
-    return lax.psum(kept, axis)
+    return jnp.sum(lax.all_gather(kept, axis), axis=0)
 
 
 def body(panel, inverse_factor, slot_rows, slot_cols, live_count):

time: 230 us -> 246 us (1.070)
  the two profiles are of different devices: /device:TPU:32 before, /device:TPU:7 now
where the time goes in v2:
time: 246 us; the launch traced here: 245 us
  waiting for transfers between devices  201 us (82%)
  between operations  13.5 us (5%)
  loops' own time  12.4 us (5%)
  other arithmetic  9.24 us (4%)
  matrix products  4.72 us (2%)
  local copies, waits for them, and re-layouts  4.43 us (2%)
    all_gather x1, waiting for transfers between devices, broadcast(): return jnp.sum(lax.all_gather(kept, axis), axis=0)  124 us
    all_gather x1, waiting for transfers between devices, body(): lax.all_gather(solved, 'col', axis=2, tiled=True)  76.8 us
    another operation x1, loops' own time, body(): result = lax.fori_loop(0, live_here, update, result)  12.4 us
    reduce_sum x1, other arithmetic, broadcast(): return jnp.sum(lax.all_gather(kept, axis), axis=0)  6.98 us
  transfers between devices with their start and end apart: 2, of which 2 were waited for; matrix products, arithmetic and copies ran while one was open for 0% of the time, Pallas kernels for 0%

profile of v2, /device:TPU:7, one launch (start us, length us, event | category | flops | bytes accessed | tf_op | source)
XLA Modules:
  0.0 245.1 jit_solution(3837040170424708912)
XLA Ops:
  6.5 0.0 copy-start
  6.5 0.0 all-gather.4.cloned.1.call-start
  6.5 1.0 copy-done
  7.6 1.7 convolution_convert_fusion
  9.3 0.0 all-gather.4.cloned.1.call-update
  9.3 0.0 all-gather.6.cloned.1.call-start
  9.4 76.8 %all-gather.4.cloned.1.call-done = bf16[4,1,512,512]{3,2,0,1:T(8,128)(2,1)} async-done(((bf16[4,1,16,512]{3,2,0,1:T(8,128)(2,1)}), bf16[4,1,512,512]{3,2,0,1:T(8,128)(2,1)}) %all-gather.4.cloned.1.call-update) | async-done | bytes 2097168 | tf_op jit(solution)/shard_map/all_gather | solution.py:22
  86.2 2.3 dynamic-slice_select_fusion
  88.5 0.0 all-gather.6.cloned.1.call-update
  88.5 123.9 %all-gather.6.cloned.1.call-done = bf16[32,1,512,512]{3,2,1,0:T(8,128)(2,1)} async-done(((bf16[2,1,512,512]{3,2,1,0:T(8,128)(2,1)}), bf16[32,1,512,512]{3,2,1,0:T(8,128)(2,1)}) %all-gather.6.cloned.1.call-update) | async-done | bytes 16777232 | tf_op jit(solution)/shard_map/all_gather | solution.py:9
  212.4 0.0 copy-start.2
  212.4 7.0 %bitcast_reduce_fusion = bf16[2,512,512]{2,1,0:T(8,128)(2,1)S(1)} fusion(bf16[16,2,512,512]{3,2,1,0:T(8,128)(2,1)} %bitcast.35), kind=kLoop, calls=%fused_computation.9 | loop fusion | flops 7864320 | bytes 17825792 | tf_op jit(solution)/shard_map/reduce_sum | solution.py:9
  219.4 0.1 broadcast_in_dim.15
  219.5 0.0 copy-done.2
  219.5 0.0 copy-done.3
  219.5 17.8 %while.13 = (s32[]{:T(128)}, bf16[2,512,512]{2,1,0:T(8,128)(2,1)S(1)}, s32[]{:T(128)}, s32[2]{0:T(128)S(1)}, bf16[4,512,512]{2,1,0:T(8,128)(2,1)}, /*index=5*/s3...) while((s32[]{:T(128)}, ...), condition=%wide.region_2.3_spmd, body=%wide.region_1.2_spmd.sunk | while | flops 268959776 | bytes 1573443 | solution.py:47
  220.1 0.6 dynamic_slice.51
  223.3 0.6 dynamic_slice.50
  226.5 1.5 fusion.15
  228.7 0.6 dynamic_slice.51
  231.9 0.6 dynamic_slice.50
  235.1 1.5 fusion.15
  237.3 0.0 copy-start.1
  237.3 1.0 copy-done.1
  (1 shorter events, 0.0 us)
Async XLA Ops:
  6.5 1.0 copy-start
  6.5 79.6 %all-gather.4.cloned.1.call-start = ((), (), s32[]{:S(2)}) async-start(), calls=%async_computation | async-start | bytes 2162688 | tf_op jit(solution)/shard_map/all_gather | solution.py:22
  9.3 203.1 %all-gather.6.cloned.1.call-start = ((), (), s32[]{:S(2)}) async-start(), calls=%async_computation.1 | async-start | bytes 17825792 | tf_op jit(solution)/shard_map/all_gather | solution.py:9
  212.4 7.1 %copy-start.2 = (s32[1,1,2]{2,1,0:T(1,128)S(1)}, s32[1,1,2]{2,1,0:T(1,128)}, u32[]{:S(2)}) copy-start(s32[1,1,2]{2,1,0:T(1,128)} %param.9) | copy-start | bytes 28
  212.4 7.1 %copy-start.3 = (s32[1,1,2]{2,1,0:T(1,128)S(1)}, s32[1,1,2]{2,1,0:T(1,128)}, u32[]{:S(2)}) copy-start(s32[1,1,2]{2,1,0:T(1,128)} %param.10) | copy-start | bytes 28
  237.3 1.0 copy-start.1
Sparse Core Ops, SparseCore 0:
  9.5 76.6 all-gather.3
  89.2 123.1 all-gather.5
